TPU v7x, 32 devices: a whole 2x2x4 slice. The times are simulated.
32 devices in a mesh: groups: 2 (over x), seq: 16 (over z, y, core).
Axes of the slice: x: 2, y: 2, z: 4, core: 2. Of those that a mesh axis runs over, the one named last changes fastest.
Arguments:
- bases: int32 [24576], P(('groups', 'seq')), parts along dimension 0, may hold values from 0 to 4
- stem_weight: bfloat16 [5, 4, 768], replicated, may hold values from -3 to 3
- weight_top: bfloat16 [5, 768, 768], P(None, None, 'seq'), may hold values from -0.09375 to 0.09375
- weight_deep: bfloat16 [5, 768, 896], P(None, None, 'seq'), may hold values from -0.09375 to 0.09375
- weight_up: bfloat16 [5, 896, 768], P(None, None, 'seq'), may hold values from -0.09375 to 0.09375
- gain_top: float32 [768], replicated, may hold values from 0.1 to 1.9
- gain_deep: float32 [768], replicated, may hold values from 0.1 to 1.9
- gain_up: float32 [896], replicated, may hold values from 0.1 to 1.9
Outputs:
- decoded: bfloat16 [24576, 768], P(('groups', 'seq')), parts along dimension 0
There are 2 independent parts, one for each index of `groups`. A program takes and returns all parts, laid end to end along the dimension named above; an argument that names none is the same for every part. Nothing has to cross between parts.
Inputs may be any that keep to these rules, and one draw needn't show every extreme that they name: 0 to 3 are the bases A, C, G, T; 4 is an unknown base.
All inputs are finite; a program needn't handle non-finite values.
Results may differ from a plain program's by a relative error of at most 0.008.
Values may be sent and summed in bfloat16 or wider, within the bound.
A program may use at most 128 MiB of HBM per device.

v0:
```python
import jax
import jax.numpy as jnp
from jax import lax
from jax.sharding import PartitionSpec as P

TAPS = 5


def with_halo(block, sides, width):
    for axis, dim in sides:
        count = lax.axis_size(axis)
        forward = [(i, i + 1) for i in range(count - 1)]
        backward = [(target, source) for source, target in forward]
        low = lax.ppermute(
            lax.slice_in_dim(block, block.shape[dim] - width, None, axis=dim), axis, forward
        )
        high = lax.ppermute(lax.slice_in_dim(block, 0, width, axis=dim), axis, backward)
        block = jnp.concatenate([low, block, high], axis=dim)
    return block


def activate(values, gain):
    wide = values.astype(jnp.float32)
    meansq = jnp.mean(wide * wide, axis=-1, keepdims=True)
    return jax.nn.gelu(wide * lax.rsqrt(meansq + 1e-06) * gain).astype(jnp.bfloat16)


def taps_conv(padded, weight):
    count = padded.shape[0] - weight.shape[0] + 1
    total = jnp.zeros((count, weight.shape[2]), jnp.float32)
    for tap in range(weight.shape[0]):
        total = total + jnp.dot(
            padded[tap : tap + count], weight[tap], preferred_element_type=jnp.float32
        )
    return total


def stem_embed(extended, stem_weight, count):
    window = jnp.stack([extended[tap : tap + count] for tap in range(TAPS)], axis=1)
    codes = jnp.arange(1, 5, dtype=jnp.int32)
    onehot = (
        (window[:, :, None] == codes[None, None, :]).astype(jnp.bfloat16).reshape(count, TAPS * 4)
    )
    table = stem_weight.reshape(TAPS * 4, stem_weight.shape[2])
    return jnp.dot(onehot, table, preferred_element_type=jnp.float32)


def per_device(
    bases, stem_weight, weight_top, weight_deep, weight_up, gain_top, gain_deep, gain_up
):
    count = bases.shape[0]
    half = count // 2
    full_top = lax.all_gather(weight_top, "seq", axis=2, tiled=True)
    extended = with_halo(bases + 1, (("seq", 0),), 2)
    embedded = stem_embed(extended, stem_weight, count).astype(jnp.bfloat16)
    act_top = with_halo(activate(embedded, gain_top), (("seq", 0),), 2)
    full_deep = lax.all_gather(weight_deep, "seq", axis=2, tiled=True)
    conv_top = taps_conv(act_top, full_top)
    skip = (embedded.astype(jnp.float32) + conv_top).astype(jnp.bfloat16)
    pooled = jnp.max(skip.reshape(half, 2, skip.shape[1]), axis=1)
    act_deep = with_halo(activate(pooled, gain_deep), (("seq", 0),), 2)
    full_up = lax.all_gather(weight_up, "seq", axis=2, tiled=True)
    conv_deep = taps_conv(act_deep, full_deep)
    widened = jnp.pad(
        pooled.astype(jnp.float32), ((0, 0), (0, conv_deep.shape[1] - pooled.shape[1]))
    )
    deep = (conv_deep + widened).astype(jnp.bfloat16)
    act_up = activate(deep, gain_up)
    raised = with_halo(jnp.repeat(act_up, 2, axis=0), (("seq", 0),), 2)
    conv_up = taps_conv(raised, full_up)
    return (conv_up + skip.astype(jnp.float32)).astype(jnp.bfloat16)


def solution(mesh):
    placed = (
        P(("groups", "seq")),
        P(),
        P(None, None, "seq"),
        P(None, None, "seq"),
        P(None, None, "seq"),
        P(),
        P(),
        P(),
    )
    return jax.shard_map(
        per_device,
        mesh=mesh,
        in_specs=placed,
        out_specs=P(("groups", "seq"), None),
        check_vma=False,
    )
```

profile of v0, /device:TPU:0, one launch (start us, length us, event | category | flops | bytes accessed | tf_op | source)
XLA Modules:
  0.0 220.4 jit_solution(1809960731546232243)
XLA Ops:
  6.5 0.0 copy-start
  6.5 0.0 all-gather.4.cloned.1.call-start
  6.5 0.7 all-gather.4.cloned.1.call-update
  7.3 0.0 all-gather.6.cloned.1.call-start
  7.3 0.7 all-gather.6.cloned.1.call-update
  8.0 0.0 all-gather.8.cloned.1.call-start
  8.1 0.7 all-gather.8.cloned.1.call-update
  8.7 0.7 broadcast_add_fusion
  9.4 0.1 fusion.82
  9.5 2.4 %collective-permute-start = (s32[2]{0:T(128)S(1)}, s32[2]{0:T(128)S(1)}, u32[]{:S(2)}, u32[]{:S(2)}) collective-permute-start(s32[2]{0:T(128)S(1)} %get-tuple-element.16), channel_id=1, source_target_pairs={{0,1},{1,2},{2,3},{3,4},{4,5},{5,6},{6,7},{7,8},{8,9},{9,10},{10,1... | collective-permute-start | bytes 32 | tf_op jit(solution)/shard_map/ppermute | solution.py:14
  11.9 1.3 collective-permute-start.1
  13.2 0.0 collective-permute-done
  13.2 3.8 %collective-permute-done.1 = s32[2]{0:T(128)S(1)} collective-permute-done((s32[2]{0:T(128)S(1)}, s32[2]{0:T(128)S(1)}, u32[]{:S(2)}, u32[]{:S(2)}) %collective-permute-start.1) | collective-permute-done | bytes 40 | tf_op jit(solution)/shard_map/ppermute | solution.py:17
  17.1 0.1 pad_add_fusion.1
  17.2 0.1 fusion.81
  17.3 0.0 copy-start.8
  17.3 0.7 fusion
  18.0 1.0 copy-done.2
  19.0 1.0 fusion.4
  20.1 4.2 %collective-permute-start.2 = (bf16[2,768]{1,0:T(2,128)(2,1)S(1)}, bf16[2,768]{1,0:T(2,128)(2,1)S(1)}, u32[]{:S(2)}, u32[]{:S(2)}) collective-permute-start(bf16[2,768]{1,0:T(2,128)(2,1)S(1)} %get-tuple-element.7), channel_id=1, source_target_pairs={{0,1},{1,2},{2,3},{3,4},{4,5},{5,6},{6,7},{7,8},{8,9},{9,10},{10,1... | collective-permute-start | bytes 9224 | tf_op jit(solution)/shard_map/ppermute | solution.py:14
  24.3 1.3 collective-permute-start.3
  25.6 0.0 collective-permute-done.2
  25.6 46.1 %all-gather.4.cloned.1.call-done = bf16[5,768,768]{1,2,0:T(8,128)(2,1)} async-done(((bf16[5,768,48]{1,2,0:T(8,128)(2,1)}), bf16[5,768,768]{1,2,0:T(8,128)(2,1)}) %all-gather.4.cloned.1.call-update) | async-done | bytes 5898256 | tf_op jit(solution)/shard_map/all_gather | solution.py:53
  71.7 2.6 %fusion.42 = f32[768,768]{1,0:T(8,128)S(1)} fusion(bf16[2,768]{1,0:T(2,128)(2,1)S(1)} %collective-permute-done.2, bf16[768,768]{1,0:T(8,128)(2,1)S(1)} %fusion.4, bf16[5,768,768]{1,2,0:T(8,128)(2,1)} %all-gather.4.cloned.1.call-done), kind=kOutput, calls=%fused_computation.69 | convolution fusion | flops 908328960 | bytes 4721664 | tf_op jit(solution)/shard_map/dot_general | solution.py:32
  74.3 0.5 copy-done.7
  74.7 1.1 fusion.55
  75.9 0.0 collective-permute-done.3
  75.9 1.1 fusion.39
  77.0 1.1 fusion.54
  78.2 0.1 copy-done.3
  78.3 1.4 fusion.9
  79.7 0.5 reshape.44
  80.2 0.0 copy-start.9
  80.2 3.2 %reduce_max.9 = bf16[384,768]{1,0:T(8,128)(2,1)S(1)} reduce(bf16[384,2,768]{2,1,0:T(2,128)(2,1)S(1)} %reshape.44, bf16[]{:T(256)} %constant.18.clone.1), dimensions={1}, to_apply=%region_1.0 | reduce | flops 294912 | bytes 1769474 | tf_op jit(solution)/shard_map/reduce_max | solution.py:60
  83.4 0.2 multiply_reduce_fusion
  83.6 0.5 fusion.51
  84.2 2.1 collective-permute-start.4
  86.4 1.1 convert_element_type.42
  87.4 1.5 collective-permute-start.5
  88.9 0.0 collective-permute-done.4
  88.9 48.6 %all-gather.6.cloned.1.call-done = bf16[5,768,896]{1,2,0:T(8,128)(2,1)} async-done(((bf16[5,768,56]{1,2,0:T(8,128)(2,1)}), bf16[5,768,896]{1,2,0:T(8,128)(2,1)}) %all-gather.6.cloned.1.call-update) | async-done | bytes 6881296 | tf_op jit(solution)/shard_map/all_gather | solution.py:57
  137.5 2.3 %fusion.36 = f32[384,896]{1,0:T(8,128)S(1)} fusion(bf16[5,768,896]{1,2,0:T(8,128)(2,1)} %all-gather.6.cloned.1.call-done, bf16[384,768]{1,0:T(8,128)(2,1)S(1)} %fusion.51, bf16[2,768]{1,0:T(2,128)(2,1)S(1)} %collective-permute-done.4), kind=kOutput, calls=%fused_computation.59 | convolution fusion | flops 529661952 | bytes 3345408 | tf_op jit(solution)/shard_map/dot_general | solution.py:32
  139.8 0.0 collective-permute-done.5
  139.8 2.2 %fusion.34 = f32[384,896]{1,0:T(8,128)S(1)} fusion(bf16[5,768,896]{1,2,0:T(8,128)(2,1)} %all-gather.6.cloned.1.call-done, bf16[2,768]{1,0:T(2,128)(2,1)S(1)} %collective-permute-done.5, bf16[384,768]{1,0:T(8,128)(2,1)S(1)} %fusion.51), kind=kOutput, calls=%fused_computation.54 | convolution fusion | flops 529661952 | bytes 3345408 | tf_op jit(solution)/shard_map/dot_general | solution.py:32
  142.0 0.8 fusion.35
  142.8 0.9 fusion.11
  143.7 0.4 copy-done.4
  144.1 1.0 fusion.17
  145.1 0.6 fusion.21
  145.7 1.8 broadcast_in_dim.2
  147.5 3.3 %reshape.45 = bf16[768,896]{1,0:T(8,128)(2,1)S(1)} reshape(bf16[384,2,896]{2,1,0:T(2,128)(2,1)} %broadcast_in_dim.2) | data formatting | bytes 2752512 | tf_op jit(solution)/shard_map/reshape | solution.py:69
  150.9 2.1 collective-permute-start.6
  153.1 1.3 collective-permute-start.7
  154.4 1.2 constant_dynamic-update-slice_fusion.1
  155.6 47.7 %all-gather.8.cloned.1.call-done = bf16[5,896,768]{1,2,0:T(8,128)(2,1)} async-done(((bf16[5,896,48]{1,2,0:T(8,128)(2,1)}), bf16[5,896,768]{1,2,0:T(8,128)(2,1)}) %all-gather.8.cloned.1.call-update) | async-done | bytes 6881296 | tf_op jit(solution)/shard_map/all_gather | solution.py:62
  203.4 2.9 %fusion.31 = f32[768,768]{1,0:T(8,128)S(1)} fusion(bf16[768,896]{1,0:T(8,128)(2,1)S(1)} %reshape.45, bf16[5,896,768]{1,2,0:T(8,128)(2,1)} %all-gather.8.cloned.1.call-done), kind=kOutput, calls=%fused_computation.47 | convolution fusion | flops 1056964608 | bytes 5111808 | tf_op jit(solution)/shard_map/dot_general | solution.py:32
  206.3 0.0 collective-permute-done.6
  206.3 0.4 copy-done.6
  206.7 1.4 fusion.15
  208.2 0.0 copy-start.1
  208.2 1.4 fusion.32
  209.6 0.0 collective-permute-done.7
  209.7 1.4 fusion.29
  211.1 2.8 %add_convert_fusion = bf16[768,768]{1,0:T(8,128)(2,1)} fusion(bf16[768,768]{1,0:T(8,128)(2,1)S(1)} %fusion.9, f32[768,768]{1,0:T(8,128)S(1)} %fusion.29, f32[768,768]{1,0:T(8,128)S(1)} %fusion.31, f32[768,768]{1,0:T(8,128)S(1)} %fusion.15, f32[768,768]{1,0:T(8,128)S(1)} %fusion.32, bf16[5,896,768]{1,2,0:T(8,128)(2,1)S(1)} %copy-done.6, ...), kind=kOutput, calls=%fused_computation.16 | convolution fusion | flops 1061093376 | bytes 14548992 | tf_op jit(solution)/shard_map/dot_general | solution.py:32
  (29 shorter events, 0.2 us)
Async XLA Ops:
  6.5 10.8 %copy-start = (bf16[5,4,768]{2,1,0:T(4,128)(2,1)S(1)}, bf16[5,4,768]{2,1,0:T(4,128)(2,1)}, u32[]{:S(2)}) copy-start(bf16[5,4,768]{2,1,0:T(4,128)(2,1)} %param.9) | copy-start | bytes 92164
  6.5 65.2 %all-gather.4.cloned.1.call-start = ((), (), s32[]{:S(2)}) async-start(), calls=%async_computation | async-start | bytes 6266880 | tf_op jit(solution)/shard_map/all_gather | solution.py:53
  7.3 130.2 %all-gather.6.cloned.1.call-start = ((), (), s32[]{:S(2)}) async-start(), calls=%async_computation.1 | async-start | bytes 7311360 | tf_op jit(solution)/shard_map/all_gather | solution.py:57
  8.0 195.3 %all-gather.8.cloned.1.call-start = ((), (), s32[]{:S(2)}) async-start(), calls=%async_computation.2 | async-start | bytes 7311360 | tf_op jit(solution)/shard_map/all_gather | solution.py:62
  9.5 3.7 %collective-permute-start = (s32[2]{0:T(128)S(1)}, s32[2]{0:T(128)S(1)}, u32[]{:S(2)}, u32[]{:S(2)}) collective-permute-start(s32[2]{0:T(128)S(1)} %get-tuple-element.16), channel_id=1, source_target_pairs={{0,1},{1,2},{2,3},{3,4},{4,5},{5,6},{6,7},{7,8},{8,9},{9,10},{10,1... | collective-permute-start | bytes 32 | tf_op jit(solution)/shard_map/ppermute | solution.py:14
  11.9 5.2 %collective-permute-start.1 = (s32[2]{0:T(128)S(1)}, s32[2]{0:T(128)S(1)}, u32[]{:S(2)}, u32[]{:S(2)}) collective-permute-start(s32[2]{0:T(128)S(1)} %get-tuple-element.15), channel_id=1, source_target_pairs={{1,0},{2,1},{3,2},{4,3},{5,4},{6,5},{7,6},{8,7},{9,8},{10,9},{11,1... | collective-permute-start | bytes 32 | tf_op jit(solution)/shard_map/ppermute | solution.py:17
  17.3 1.7 copy-start.8
  18.0 1.0 copy-start.2
  20.1 5.5 %collective-permute-start.2 = (bf16[2,768]{1,0:T(2,128)(2,1)S(1)}, bf16[2,768]{1,0:T(2,128)(2,1)S(1)}, u32[]{:S(2)}, u32[]{:S(2)}) collective-permute-start(bf16[2,768]{1,0:T(2,128)(2,1)S(1)} %get-tuple-element.7), channel_id=1, source_target_pairs={{0,1},{1,2},{2,3},{3,4},{4,5},{5,6},{6,7},{7,8},{8,9},{9,10},{10,1... | collective-permute-start | bytes 9224 | tf_op jit(solution)/shard_map/ppermute | solution.py:14
  24.3 51.6 %collective-permute-start.3 = (bf16[2,768]{1,0:T(2,128)(2,1)S(1)}, bf16[2,768]{1,0:T(2,128)(2,1)S(1)}, u32[]{:S(2)}, u32[]{:S(2)}) collective-permute-start(bf16[2,768]{1,0:T(2,128)(2,1)S(1)} %get-tuple-element.8), channel_id=1, source_target_pairs={{1,0},{2,1},{3,2},{4,3},{5,4},{6,5},{7,6},{8,7},{9,8},{10,9},{11,1... | collective-permute-start | bytes 9224 | tf_op jit(solution)/shard_map/ppermute | solution.py:17
  71.7 3.0 %copy-start.7 = (bf16[5,768,768]{1,2,0:T(8,128)(2,1)S(1)}, bf16[5,768,768]{1,2,0:T(8,128)(2,1)}, u32[]{:S(2)}) copy-start(bf16[5,768,768]{1,2,0:T(8,128)(2,1)} %all-gather.4.cloned.1.call-done) | copy-start | bytes 17694724
  77.0 1.3 copy-start.3
  80.2 3.4 %copy-start.9 = (f32[768]{0:T(1024)S(1)}, f32[768]{0:T(1024)}, u32[]{:S(2)}) copy-start(f32[768]{0:T(1024)} %param.14) | copy-start | bytes 9220
  84.2 4.7 %collective-permute-start.4 = (bf16[2,768]{1,0:T(2,128)(2,1)S(1)}, bf16[2,768]{1,0:T(2,128)(2,1)S(1)}, u32[]{:S(2)}, u32[]{:S(2)}) collective-permute-start(bf16[2,768]{1,0:T(2,128)(2,1)S(1)} %get-tuple-element.9), channel_id=1, source_target_pairs={{0,1},{1,2},{2,3},{3,4},{4,5},{5,6},{6,7},{7,8},{8,9},{9,10},{10,1... | collective-permute-start | bytes 9224 | tf_op jit(solution)/shard_map/ppermute | solution.py:14
  87.4 52.3 %collective-permute-start.5 = (bf16[2,768]{1,0:T(2,128)(2,1)S(1)}, bf16[2,768]{1,0:T(2,128)(2,1)S(1)}, u32[]{:S(2)}, u32[]{:S(2)}) collective-permute-start(bf16[2,768]{1,0:T(2,128)(2,1)S(1)} %get-tuple-element.10), channel_id=1, source_target_pairs={{1,0},{2,1},{3,2},{4,3},{5,4},{6,5},{7,6},{8,7},{9,8},{10,9},{11,1... | collective-permute-start | bytes 9224 | tf_op jit(solution)/shard_map/ppermute | solution.py:17
  137.5 4.5 %copy-start.5 = (bf16[5,768,896]{1,2,0:T(8,128)(2,1)S(1)}, bf16[5,768,896]{1,2,0:T(8,128)(2,1)}, u32[]{:S(2)}) copy-start(bf16[5,768,896]{1,2,0:T(8,128)(2,1)} %all-gather.6.cloned.1.call-done) | copy-start | bytes 20643844
  142.8 1.3 copy-start.4
  144.1 1.0 copy-start.10
  150.9 55.4 %collective-permute-start.6 = (bf16[2,896]{1,0:T(2,128)(2,1)S(1)}, bf16[2,896]{1,0:T(2,128)(2,1)S(1)}, u32[]{:S(2)}, u32[]{:S(2)}) collective-permute-start(bf16[2,896]{1,0:T(2,128)(2,1)S(1)} %slice.175), channel_id=1, source_target_pairs={{0,1},{1,2},{2,3},{3,4},{4,5},{5,6},{6,7},{7,8},{8,9},{9,10},{10,1... | collective-permute-start | bytes 10760 | tf_op jit(solution)/shard_map/ppermute | solution.py:14
  153.1 56.5 %collective-permute-start.7 = (bf16[2,896]{1,0:T(2,128)(2,1)S(1)}, bf16[2,896]{1,0:T(2,128)(2,1)S(1)}, u32[]{:S(2)}, u32[]{:S(2)}) collective-permute-start(bf16[2,896]{1,0:T(2,128)(2,1)S(1)} %slice.183), channel_id=1, source_target_pairs={{1,0},{2,1},{3,2},{4,3},{5,4},{6,5},{7,6},{8,7},{9,8},{10,9},{11,1... | collective-permute-start | bytes 10760 | tf_op jit(solution)/shard_map/ppermute | solution.py:17
  203.4 3.4 %copy-start.6 = (bf16[5,896,768]{1,2,0:T(8,128)(2,1)S(1)}, bf16[5,896,768]{1,2,0:T(8,128)(2,1)}, u32[]{:S(2)}) copy-start(bf16[5,896,768]{1,2,0:T(8,128)(2,1)} %all-gather.8.cloned.1.call-done) | copy-start | bytes 20643844
  208.2 1.5 copy-start.1
Sparse Core Ops, SparseCore 0:
  9.6 62.0 all-gather.3
  73.9 63.5 all-gather.5
  139.7 63.6 all-gather.7
where the time goes:
time: 221 us; the launch traced here: 220 us
  waiting for transfers between devices  148 us (67%)
  matrix products  25.2 us (11%)
  starting transfers between devices  16.3 us (7%)
  between operations  13.5 us (6%)
  local copies, waits for them, and re-layouts  9.62 us (4%)
  other arithmetic  7.45 us (3%)
    all_gather x1, waiting for transfers between devices, per_device(): full_deep = lax.all_gather(weight_deep, 'seq', axis=2, tiled=True)  48.6 us
    all_gather x1, waiting for transfers between devices, per_device(): full_up = lax.all_gather(weight_up, 'seq', axis=2, tiled=True)  47.7 us
    all_gather x1, waiting for transfers between devices, per_device(): full_top = lax.all_gather(weight_top, 'seq', axis=2, tiled=True)  46.1 us
    dot_general x15, matrix products, taps_conv(): jnp.dot(padded[tap:tap + count], weight[tap], preferred_element_type=jnp....  24.5 us
    ppermute x4, starting transfers between devices, with_halo(): lax.ppermute(lax.slice_in_dim(block, block.shape[dim] - width, None, axis...  10.9 us
    ppermute x4, starting transfers between devices, with_halo(): lax.ppermute(lax.slice_in_dim(block, 0, width, axis=dim), axis, backward)  5.34 us
  transfers between devices with their start and end apart: 11, of which 4 were waited for; matrix products, arithmetic and copies ran while one was open for 16% of the time, Pallas kernels for 0%

commit v1 on v0

--- a/solution.py
+++ b/solution.py
@@ -1,6 +1,10 @@
+import functools
+
 import jax
 import jax.numpy as jnp
 from jax import lax
+from jax.experimental import pallas as pl
+from jax.experimental.pallas import tpu as pltpu
 from jax.sharding import PartitionSpec as P
 
 TAPS = 5
@@ -71,7 +75,380 @@
     return (conv_up + skip.astype(jnp.float32)).astype(jnp.bfloat16)
 
 
+MESH = pl.DeviceIdType.MESH
+EDGE = 8
+CHUNK = 80
+
+
+def fused_kernel(
+    nz,
+    half,
+    onehot_ref,
+    table_ref,
+    top_ref,
+    deep_ref,
+    up_ref,
+    gain_top_ref,
+    gain_deep_ref,
+    gain_up_ref,
+    out_ref,
+    full_top,
+    full_deep,
+    full_up,
+    flat_deep,
+    even_up,
+    odd_up,
+    wide,
+    embedded,
+    skip,
+    cols_top,
+    cols_deep,
+    cols_up,
+    send_sem,
+    recv_sem,
+    own_sem,
+):
+    g = lax.axis_index("groups")
+    s = lax.axis_index("seq")
+    core, y, z = s % 2, (s // 2) % 2, s // 4
+    rows = half + 2 * EDGE
+    c0 = embedded.shape[1]
+    c1 = deep_ref.shape[0] * (4 * nz)
+    own_refs = (top_ref, deep_ref, up_ref)
+    widths = tuple(ref.shape[1] // 2 for ref in own_refs)
+
+    def index(z_at, y_at, core_at):
+        return z_at * 4 + y_at * 2 + core_at
+
+    def away(k):
+        return lax.rem(z + k, nz)
+
+    mirror = (1 - g, s)
+    across = (g, index(z, 1 - y, core))
+    sibling = (g, index(z, y, 1 - core))
+
+    barrier = pltpu.get_barrier_semaphore()
+    partners = [mirror, across, sibling] + [
+        (g, index(away(k), y, core)) for k in range(1, nz)
+    ]
+    for partner in partners:
+        pl.semaphore_signal(barrier, inc=1, device_id=partner, device_id_type=MESH)
+    pl.semaphore_wait(barrier, len(partners))
+
+    def columns(stage, h):
+        return pl.ds(pl.multiple_of(h * widths[stage], 128), widths[stage])
+
+    def place(stage, h, at):
+        cols = columns(stage, h)
+        if stage == 1:
+            return full_deep.at[at, :, cols]
+        depth = own_refs[stage].shape[0]
+        ref = full_top if stage == 0 else full_up
+        return ref.at[pl.ds(pl.multiple_of(at * depth, 16), depth), cols]
+
+    started = []
+
+    def send(stage, h, at, device, own=False):
+        source = own_refs[stage].at[:, columns(stage, h)] if own else place(stage, h, at)
+        copy = pltpu.make_async_remote_copy(
+            src_ref=source,
+            dst_ref=place(stage, h, at),
+            send_sem=send_sem.at[len(started)],
+            recv_sem=recv_sem.at[stage, h, at],
+            device_id=device,
+            device_id_type=MESH,
+        )
+        copy.start()
+        started.append(copy)
+
+    def arrive(stage, h, at):
+        pltpu.make_async_remote_copy(
+            src_ref=place(stage, h, at),
+            dst_ref=place(stage, h, at),
+            send_sem=send_sem.at[0],
+            recv_sem=recv_sem.at[stage, h, at],
+            device_id=sibling,
+            device_id_type=MESH,
+        ).wait_recv()
+
+    via_mirror = [k for k in range(1, nz) if k % 3 != 0]
+    own_copies = []
+
+    def begin(stage):
+        for k in range(1, nz):
+            send(stage, g, s, (g, index(away(k), y, core)), own=True)
+        for h in (g, 1 - g):
+            send(stage, h, s, across, own=True)
+            send(stage, h, s, sibling, own=True)
+        depth = own_refs[stage].shape[0]
+        if stage == 1:
+            target = full_deep.at[s]
+        else:
+            ref = full_top if stage == 0 else full_up
+            target = ref.at[pl.ds(pl.multiple_of(s * depth, 16), depth)]
+        copy = pltpu.make_async_copy(own_refs[stage], target, own_sem.at[stage])
+        copy.start()
+        own_copies.append(copy)
+
+    def first(stage):
+        for k in range(1, nz):
+            at = index(away(k), y, core)
+            arrive(stage, g, at)
+            send(stage, g, at, mirror)
+            send(stage, g, at, across)
+            send(stage, g, at, sibling)
+
+    def second(stage):
+        for h in (g, 1 - g):
+            at = index(z, 1 - y, core)
+            arrive(stage, h, at)
+            send(stage, h, at, sibling)
+        for k in range(1, nz):
+            at = index(away(k), 1 - y, core)
+            arrive(stage, g, at)
+            if k in via_mirror:
+                send(stage, g, at, mirror)
+            send(stage, g, at, sibling)
+            at = index(away(k), y, core)
+            arrive(stage, 1 - g, at)
+            if k not in via_mirror:
+                send(stage, 1 - g, at, across)
+            send(stage, 1 - g, at, sibling)
+
+    def third(stage):
+        for k in range(1, nz):
+            at = index(away(k), 1 - y, core)
+            arrive(stage, 1 - g, at)
+            send(stage, 1 - g, at, sibling)
+
+    def last(stage):
+        for h in (0, 1):
+            for k in range(nz):
+                for y_at in (0, 1):
+                    arrive(stage, h, index(away(k), y_at, 1 - core))
+        own_copies[stage].wait()
+
+    chunks = range(0, rows, CHUNK)
+
+    def act_rows(values, gain_ref, start):
+        meansq = jnp.mean(values * values, axis=-1, keepdims=True)
+        result = jax.nn.gelu(values * lax.rsqrt(meansq + 1e-06) * gain_ref[...])
+        at = lax.broadcasted_iota(jnp.int32, (values.shape[0], 1), 0) + (
+            s * half + start - EDGE
+        )
+        inside = (at >= 0) & (at < 4 * nz * half)
+        return jnp.where(inside, result, 0.0)
+
+    def prepare_top():
+        for parity in range(2):
+            for start in chunks:
+                at = parity * rows + start
+                value = jnp.dot(
+                    onehot_ref[at : at + CHUNK, :],
+                    table_ref[...],
+                    preferred_element_type=jnp.float32,
+                ).astype(jnp.bfloat16)
+                embedded[at : at + CHUNK, :] = value
+                wide[parity, EDGE + start : EDGE + start + CHUNK, :c0] = act_rows(
+                    value.astype(jnp.float32), gain_top_ref, start
+                )
+        for start in chunks:
+            for parity in range(2):
+                for tap in range(TAPS):
+                    moved = parity + tap - 2
+                    low = EDGE + start + moved // 2
+                    cols_top[
+                        parity * rows + start : parity * rows + start + CHUNK,
+                        tap * c0 : (tap + 1) * c0,
+                    ] = wide[moved % 2, low : low + CHUNK, :c0].astype(jnp.bfloat16)
+
+    def dot_nt(a, b):
+        return lax.dot_general(
+            a, b, (((1,), (1,)), ((), ())), preferred_element_type=jnp.float32
+        )
+
+    def compute_top():
+        @pl.loop(0, c0 // 256)
+        def _(n):
+            at = pl.ds(pl.multiple_of(n * 256, 256), 256)
+            conv = dot_nt(cols_top[...], full_top[at, :])
+            skip[:, at] = (
+                (embedded[:, at].astype(jnp.float32) + conv)
+                .astype(jnp.bfloat16)
+                .astype(jnp.float32)
+            )
+
+        for start in chunks:
+            pooled = jnp.maximum(
+                skip[start : start + CHUNK, :], skip[rows + start : rows + start + CHUNK, :]
+            )
+            wide[0, EDGE + start : EDGE + start + CHUNK, :c0] = act_rows(
+                pooled, gain_deep_ref, start
+            )
+        for start in chunks:
+            for tap in range(TAPS):
+                low = EDGE + start + tap - 2
+                cols_deep[start : start + CHUNK, tap * c0 : (tap + 1) * c0] = wide[
+                    0, low : low + CHUNK, :c0
+                ].astype(jnp.bfloat16)
+
+    def compute_deep():
+        depth = deep_ref.shape[0]
+        for at in range(4 * nz):
+            flat_deep[at * depth : (at + 1) * depth, :] = full_deep[at]
+        for low in range(0, c1, 256):
+            high = min(low + 256, c1)
+            conv = dot_nt(cols_deep[...], flat_deep[low:high, :])
+            if low < c0:
+                conv = conv + jnp.maximum(skip[:rows, low:high], skip[rows:, low:high])
+            wide[1, EDGE : EDGE + rows, low:high] = conv.astype(jnp.bfloat16).astype(
+                jnp.float32
+            )
+        for start in chunks:
+            at = slice(EDGE + start, EDGE + start + CHUNK)
+            wide[0, at, :] = act_rows(wide[1, at, :], gain_up_ref, start)
+        for start in range(0, half, 96):
+            for tap in range(3):
+                low = 2 * EDGE + start + tap - 1
+                cols_up[start : start + 96, tap * c1 : (tap + 1) * c1] = wide[
+                    0, low : low + 96, :
+                ].astype(jnp.bfloat16)
+
+    def compute_up():
+        def tap_of(at, tap):
+            return full_up[at, tap * c1 : (tap + 1) * c1].astype(jnp.float32)
+
+        @pl.loop(0, c0 // 32)
+        def _(n):
+            at = pl.ds(pl.multiple_of(n * 32, 32), 32)
+            taps = [tap_of(at, tap) for tap in range(TAPS)]
+            evens = (taps[0] + taps[1], taps[2] + taps[3], taps[4])
+            odds = (taps[0], taps[1] + taps[2], taps[3] + taps[4])
+            for k in range(3):
+                even_up[at, k * c1 : (k + 1) * c1] = evens[k].astype(jnp.bfloat16)
+                odd_up[at, k * c1 : (k + 1) * c1] = odds[k].astype(jnp.bfloat16)
+
+        @pl.loop(0, c0 // 256)
+        def _(n):
+            at = pl.ds(pl.multiple_of(n * 256, 256), 256)
+            for parity, weight in enumerate((even_up, odd_up)):
+                conv = dot_nt(cols_up[...], weight[at, :])
+                low = parity * rows + EDGE
+                out_ref[:, pl.ds(pl.multiple_of(parity * c0 + n * 256, 256), 256)] = (
+                    conv + skip[low : low + half, at]
+                ).astype(jnp.bfloat16)
+
+    begin(0)
+    begin(1)
+    begin(2)
+    wide[...] = jnp.zeros_like(wide)
+    prepare_top()
+    first(0)
+    second(0)
+    first(1)
+    third(0)
+    last(0)
+    compute_top()
+    second(1)
+    first(2)
+    third(1)
+    last(1)
+    compute_deep()
+    second(2)
+    third(2)
+    last(2)
+    compute_up()
+    for copy in started:
+        copy.wait_send()
+
+
+def fused_device(
+    bases, stem_weight, weight_top, weight_deep, weight_up, gain_top, gain_deep, gain_up
+):
+    count = bases.shape[0]
+    half = count // 2
+    rows = half + 2 * EDGE
+    members = lax.axis_size("seq")
+    nz = members // 4
+    c0 = stem_weight.shape[2]
+    c1 = weight_up.shape[1]
+    bf16, f32 = jnp.bfloat16, jnp.float32
+
+    def turned(weight, lanes):
+        flat = weight.transpose(2, 0, 1).reshape(weight.shape[2], -1)
+        return jnp.pad(flat, ((0, 0), (0, -flat.shape[1] % lanes)))
+
+    shards = [turned(weight, 256) for weight in (weight_top, weight_deep, weight_up)]
+    extended = with_halo(bases + 1, (("seq", 0),), 2 * EDGE + 2)
+    pairs = extended.reshape(rows + 2, 2)
+    window = jnp.stack(
+        [
+            jnp.stack(
+                [pairs[u // 2 : u // 2 + rows, u % 2] for u in range(q, q + TAPS)], axis=1
+            )
+            for q in range(2)
+        ]
+    )
+    codes = jnp.arange(1, 5, dtype=jnp.int32)
+    onehot = (window[..., None] == codes).astype(bf16).reshape(2 * rows, TAPS * 4)
+    onehot = jnp.pad(onehot, ((0, 0), (0, 128 - TAPS * 4)))
+    table = jnp.pad(stem_weight.reshape(TAPS * 4, c0), ((0, 128 - TAPS * 4), (0, 0)))
+
+    k0, k1, k2 = (shard.shape[1] for shard in shards)
+    sends = 3 * (nz - 1 + 4 + 3 * (nz - 1) + 2 + 3 * (nz - 1) + nz - 1)
+    out = pl.pallas_call(
+        functools.partial(fused_kernel, nz, half),
+        out_shape=jax.ShapeDtypeStruct((half, 2 * c0), bf16),
+        in_specs=[pl.BlockSpec(memory_space=pltpu.VMEM)] * 8,
+        out_specs=pl.BlockSpec(memory_space=pltpu.VMEM),
+        scratch_shapes=[
+            pltpu.VMEM((c0, k0), bf16),
+            pltpu.VMEM((members, weight_deep.shape[2], k1), bf16),
+            pltpu.VMEM((c0, k2), bf16),
+            pltpu.VMEM((c1, k1), bf16),
+            pltpu.VMEM((c0, 3 * c1), bf16),
+            pltpu.VMEM((c0, 3 * c1), bf16),
+            pltpu.VMEM((2, rows + 2 * EDGE, c1), f32),
+            pltpu.VMEM((2 * rows, c0), bf16),
+            pltpu.VMEM((2 * rows, c0), f32),
+            pltpu.VMEM((2 * rows, k0), bf16),
+            pltpu.VMEM((rows, k1), bf16),
+            pltpu.VMEM((half, 3 * c1), bf16),
+            pltpu.SemaphoreType.DMA((sends,)),
+            pltpu.SemaphoreType.DMA((3, 2, members)),
+            pltpu.SemaphoreType.DMA((3,)),
+        ],
+        compiler_params=pltpu.CompilerParams(
+            collective_id=0, has_side_effects=True, vmem_limit_bytes=67043328
+        ),
+    )(
+        onehot,
+        table,
+        *shards,
+        gain_top.reshape(1, c0),
+        gain_deep.reshape(1, c0),
+        gain_up.reshape(1, c1),
+    )
+    return out.reshape(count, c0)
+
+
 def solution(mesh):
+    members = mesh.shape["seq"]
+
+    def device_step(*args):
+        bases, stem_weight, weight_top, _, weight_up, *_ = args
+        fits = (
+            mesh.shape["groups"] == 2
+            and members % 4 == 0
+            and members > 4
+            and weight_top.shape[2] % 16 == 0
+            and weight_up.shape[2] % 16 == 0
+            and stem_weight.shape[2] % 256 == 0
+            and (bases.shape[0] // 2 + 2 * EDGE) % CHUNK == 0
+            and bases.shape[0] % 192 == 0
+        )
+        return (fused_device if fits else per_device)(*args)
+
     placed = (
         P(("groups", "seq")),
         P(),
@@ -83,7 +460,7 @@
         P(),
     )
     return jax.shard_map(
-        per_device,
+        device_step,
         mesh=mesh,
         in_specs=placed,
         out_specs=P(("groups", "seq"), None),

time: 221 us -> 131 us (0.59)
  the two profiles are of different devices: /device:TPU:0 before, /device:TPU:9 now
where the time goes in v1:
time: 131 us; the launch traced here: 130 us
  Pallas kernels  108 us (82%)
  local copies, waits for them, and re-layouts  14.6 us (11%)
  starting transfers between devices  5.62 us (4%)
  other arithmetic  1.69 us (1%)
    pallas_call x1, Pallas kernels, fused_device(): pl.pallas_call(functools.partial(fused_kernel, nz, half), out_shape=jax.S...  108 us
    ppermute x1, starting transfers between devices, with_halo(): lax.ppermute(lax.slice_in_dim(block, block.shape[dim] - width, None, axis...  3.7 us
    reshape x3, local copies, waits for them, and re-layouts, turned(): flat = weight.transpose(2, 0, 1).reshape(weight.shape[2], -1)  3.61 us
    reshape x1, local copies, waits for them, and re-layouts, fused_device(): return out.reshape(count, c0)  2.95 us
  transfers between devices with their start and end apart: 2, of which 0 were waited for; matrix products, arithmetic and copies ran while one was open for 7% of the time, Pallas kernels for 0%

profile of v1, /device:TPU:9, one launch (start us, length us, event | category | flops | bytes accessed | tf_op | source)
XLA Modules:
  0.0 130.2 jit_solution(18136151335321069162)
XLA Ops:
  0.0 0.0 copy-start
  0.0 0.7 broadcast_add_fusion
  0.7 0.1 fusion.2
  0.8 3.7 %collective-permute-start = (s32[18]{0:T(128)S(1)}, s32[18]{0:T(128)S(1)}, u32[]{:S(2)}, u32[]{:S(2)}) collective-permute-start(s32[18]{0:T(128)S(1)} %get-tuple-element.12), channel_id=1, source_target_pairs={{0,1},{1,2},{2,3},{3,4},{4,5},{5,6},{6,7},{7,8},{8,9},{9,10},{10,1... | collective-permute-start | bytes 224 | tf_op jit(solution)/shard_map/ppermute | solution.py:18
  4.5 1.9 %collective-permute-start.1 = (s32[18]{0:T(128)S(1)}, s32[18]{0:T(128)S(1)}, u32[]{:S(2)}, u32[]{:S(2)}) collective-permute-start(s32[18]{0:T(128)S(1)} %get-tuple-element.13), channel_id=1, source_target_pairs={{1,0},{2,1},{3,2},{4,3},{5,4},{6,5},{7,6},{8,7},{9,8},{10,9},{11,1... | collective-permute-start | bytes 224 | tf_op jit(solution)/shard_map/ppermute | solution.py:21
  6.5 1.3 reshape.62.gain_top_ref
  7.7 1.3 reshape.63.gain_deep_ref
  9.0 0.1 eq.23
  9.1 1.3 reshape.64.gain_up_ref
  10.4 0.8 reshape.58
  11.1 1.8 %copy.42 = bf16[5,6,8,768]{3,2,0,1:T(8,128)(2,1)} copy(bf16[5,6,8,768]{3,2,1,0:T(8,128)(2,1)} %bitcast.20) | data formatting | bytes 737280 | tf_op jit(solution)/shard_map/reshape | solution.py:378
  12.9 1.8 %copy.43 = bf16[5,7,8,768]{3,2,0,1:T(8,128)(2,1)} copy(bf16[5,7,8,768]{3,2,1,0:T(8,128)(2,1)} %bitcast.18) | data formatting | bytes 860160 | tf_op jit(solution)/shard_map/reshape | solution.py:378
  14.7 0.0 copy-done
  14.7 0.7 pad.16.table_ref
  15.4 0.8 pad.17.up_ref
  16.2 0.0 collective-permute-done
  16.2 0.0 collective-permute-done.1
  16.2 0.1 pad_add_fusion.1
  16.3 0.1 fusion.1
  16.4 0.2 reshape.57
  16.6 0.2 slice.61
  16.7 0.1 copy.29
  16.8 0.2 slice.67
  17.0 0.1 copy.34
  17.1 0.2 slice.63
  17.3 0.1 copy.30
  17.4 0.1 fusion
  17.6 0.1 copy.31
  17.7 0.1 copy.32
  17.9 0.1 eq.21
  18.1 0.2 copy.37
  18.3 0.1 broadcast_compare_fusion
  18.3 0.8 pad_convert_fusion.onehot_ref
  19.1 108.2 %shard_map.82 = bf16[384,1536]{1,0:T(8,128)(2,1)} custom-call(bf16[800,128]{1,0:T(8,128)(2,1)} %pad_convert_fusion.onehot_ref, bf16[128,768]{1,0:T(8,128)(2,1)} %pad.16.table_ref, bf16[48,3840]{1,0:T(8,128)(2,1)} %bitcast.17, bf16[56,3840]{1,0:T(8,128)(2,1)} %bitcast.15, bf16[48,4608]{1,0:T(8,128)(2,1)} %pad.17.up_ref, f32[1,768]{1,0:T(1,128)} %reshape.62.gain_top_ref, ...), custom_call_target="tpu_custom_call" | custom-call | tf_op jit(solution)/shard_map/pallas_call | solution.py:399
  127.3 2.9 %reshape.65 = bf16[768,768]{1,0:T(8,128)(2,1)} reshape(bf16[384,1536]{1,0:T(8,128)(2,1)} %shard_map.82) | data formatting | bytes 2359296 | tf_op jit(solution)/shard_map/reshape | solution.py:432
  (8 shorter events, 0.1 us)
Async XLA Ops:
  0.0 14.7 %copy-start = (bf16[5,896,48]{1,2,0:T(8,128)(2,1)S(1)}, bf16[5,896,48]{1,2,0:T(8,128)(2,1)}, u32[]{:S(2)}) copy-start(bf16[5,896,48]{1,2,0:T(8,128)(2,1)} %param.12) | copy-start | bytes 1290244
  0.8 15.4 %collective-permute-start = (s32[18]{0:T(128)S(1)}, s32[18]{0:T(128)S(1)}, u32[]{:S(2)}, u32[]{:S(2)}) collective-permute-start(s32[18]{0:T(128)S(1)} %get-tuple-element.12), channel_id=1, source_target_pairs={{0,1},{1,2},{2,3},{3,4},{4,5},{5,6},{6,7},{7,8},{8,9},{9,10},{10,1... | collective-permute-start | bytes 224 | tf_op jit(solution)/shard_map/ppermute | solution.py:18
  4.5 11.7 %collective-permute-start.1 = (s32[18]{0:T(128)S(1)}, s32[18]{0:T(128)S(1)}, u32[]{:S(2)}, u32[]{:S(2)}) collective-permute-start(s32[18]{0:T(128)S(1)} %get-tuple-element.13), channel_id=1, source_target_pairs={{1,0},{2,1},{3,2},{4,3},{5,4},{6,5},{7,6},{8,7},{9,8},{10,9},{11,1... | collective-permute-start | bytes 224 | tf_op jit(solution)/shard_map/ppermute | solution.py:21

commit v2 on v1

--- a/solution.py
+++ b/solution.py
@@ -83,8 +83,8 @@
 def fused_kernel(
     nz,
     half,
-    onehot_ref,
-    table_ref,
+    hot_ref,
+    stem_ref,
     top_ref,
     deep_ref,
     up_ref,
@@ -92,6 +92,8 @@
     gain_deep_ref,
     gain_up_ref,
     out_ref,
+    hot,
+    table,
     full_top,
     full_deep,
     full_up,
@@ -107,6 +109,7 @@
     send_sem,
     recv_sem,
     own_sem,
+    hot_sem,
 ):
     g = lax.axis_index("groups")
     s = lax.axis_index("seq")
@@ -128,7 +131,10 @@
     sibling = (g, index(z, y, 1 - core))
 
     barrier = pltpu.get_barrier_semaphore()
-    partners = [mirror, across, sibling] + [
+    before, after = (
+        (g, lax.rem(s + step + 4 * nz, 4 * nz)) for step in (-1, 1)
+    )
+    partners = [mirror, across, sibling, before, after] + [
         (g, index(away(k), y, core)) for k in range(1, nz)
     ]
     for partner in partners:
@@ -146,9 +152,33 @@
         ref = full_top if stage == 0 else full_up
         return ref.at[pl.ds(pl.multiple_of(at * depth, 16), depth), cols]
 
+    edge = 2 * EDGE
+    hot_in = pltpu.make_async_copy(
+        hot_ref, hot.at[:, pl.ds(edge, half)], hot_sem.at[4]
+    )
+    hot_in.start()
+    hot_moves = [
+        pltpu.make_async_remote_copy(
+            src_ref=hot_ref.at[:, pl.ds(low, edge)],
+            dst_ref=hot.at[:, pl.ds(to, edge)],
+            send_sem=hot_sem.at[2 * n],
+            recv_sem=hot_sem.at[2 * n + 1],
+            device_id=device,
+            device_id_type=MESH,
+        )
+        for n, (low, to, device) in enumerate(
+            ((half - edge, 0, after), (0, half + edge, before))
+        )
+    ]
+    for copy in hot_moves:
+        copy.start()
+
     started = []
 
-    def send(stage, h, at, device, own=False):
+    def near(k):
+        return (k == 1) & (z < nz - 1) | (k == nz - 1) & (z > 0)
+
+    def send(stage, h, at, device, own=False, when=True):
         source = own_refs[stage].at[:, columns(stage, h)] if own else place(stage, h, at)
         copy = pltpu.make_async_remote_copy(
             src_ref=source,
@@ -158,8 +188,11 @@
             device_id=device,
             device_id_type=MESH,
         )
-        copy.start()
-        started.append(copy)
+        started.append((copy, when))
+        if when is True:
+            copy.start()
+        else:
+            pl.when(when)(copy.start)
 
     def arrive(stage, h, at):
         pltpu.make_async_remote_copy(
@@ -171,12 +204,14 @@
             device_id_type=MESH,
         ).wait_recv()
 
-    via_mirror = [k for k in range(1, nz) if k % 3 != 0]
     own_copies = []
 
     def begin(stage):
         for k in range(1, nz):
-            send(stage, g, s, (g, index(away(k), y, core)), own=True)
+            target = (g, index(away(k), y, core))
+            send(stage, g, s, target, own=True)
+            if k in (1, nz - 1):
+                send(stage, 1 - g, s, target, own=True, when=near(k))
         for h in (g, 1 - g):
             send(stage, h, s, across, own=True)
             send(stage, h, s, sibling, own=True)
@@ -194,7 +229,10 @@
         for k in range(1, nz):
             at = index(away(k), y, core)
             arrive(stage, g, at)
-            send(stage, g, at, mirror)
+            if k in (1, nz - 1):
+                send(stage, g, at, mirror, when=jnp.logical_not(near(k)))
+            else:
+                send(stage, g, at, mirror)
             send(stage, g, at, across)
             send(stage, g, at, sibling)
 
@@ -206,13 +244,10 @@
         for k in range(1, nz):
             at = index(away(k), 1 - y, core)
             arrive(stage, g, at)
-            if k in via_mirror:
-                send(stage, g, at, mirror)
+            send(stage, g, at, mirror)
             send(stage, g, at, sibling)
             at = index(away(k), y, core)
             arrive(stage, 1 - g, at)
-            if k not in via_mirror:
-                send(stage, 1 - g, at, across)
             send(stage, 1 - g, at, sibling)
 
     def third(stage):
@@ -239,14 +274,31 @@
         inside = (at >= 0) & (at < 4 * nz * half)
         return jnp.where(inside, result, 0.0)
 
+    def window(parity, start):
+        lane = lax.broadcasted_iota(jnp.int32, (CHUNK, 128), 1)
+        row = lax.broadcasted_iota(jnp.int32, (CHUNK, 128), 0)
+        total = jnp.zeros((CHUNK, 128), jnp.float32)
+        for tap in range(TAPS):
+            moved = parity + tap - 2
+            low = start + EDGE + moved // 2
+            at = s * half + start - EDGE + moved // 2 + row
+            taken = (lane // 8 == tap) & (at >= 0) & (at < 4 * nz * half)
+            total = total + jnp.where(taken, hot[moved % 2, low : low + CHUNK, :], 0.0)
+        return total.astype(jnp.bfloat16)
+
     def prepare_top():
+        table[...] = jnp.zeros_like(table)
+        for tap in range(TAPS):
+            table[tap * 8 : tap * 8 + 4, :] = stem_ref[tap].astype(jnp.float32)
+        for copy in hot_moves:
+            copy.wait()
+        hot_in.wait()
+        rows_of = table[...].astype(jnp.bfloat16)
         for parity in range(2):
             for start in chunks:
                 at = parity * rows + start
                 value = jnp.dot(
-                    onehot_ref[at : at + CHUNK, :],
-                    table_ref[...],
-                    preferred_element_type=jnp.float32,
+                    window(parity, start), rows_of, preferred_element_type=jnp.float32
                 ).astype(jnp.bfloat16)
                 embedded[at : at + CHUNK, :] = value
                 wide[parity, EDGE + start : EDGE + start + CHUNK, :c0] = act_rows(
@@ -314,20 +366,36 @@
                     0, low : low + 96, :
                 ].astype(jnp.bfloat16)
 
-    def compute_up():
-        def tap_of(at, tap):
-            return full_up[at, tap * c1 : (tap + 1) * c1].astype(jnp.float32)
-
-        @pl.loop(0, c0 // 32)
-        def _(n):
-            at = pl.ds(pl.multiple_of(n * 32, 32), 32)
-            taps = [tap_of(at, tap) for tap in range(TAPS)]
+    depth_up = up_ref.shape[0]
+
+    def sum_taps(member):
+        for part in range(0, depth_up, 16):
+            at = pl.ds(pl.multiple_of(member * depth_up + part, 16), 16)
+            taps = [
+                full_up[at, tap * c1 : (tap + 1) * c1].astype(jnp.float32)
+                for tap in range(TAPS)
+            ]
             evens = (taps[0] + taps[1], taps[2] + taps[3], taps[4])
             odds = (taps[0], taps[1] + taps[2], taps[3] + taps[4])
             for k in range(3):
                 even_up[at, k * c1 : (k + 1) * c1] = evens[k].astype(jnp.bfloat16)
                 odd_up[at, k * c1 : (k + 1) * c1] = odds[k].astype(jnp.bfloat16)
 
+    def last_up():
+        own_copies[2].wait()
+
+        @pl.loop(0, 2 * nz)
+        def _(n):
+            sum_taps(index(lax.rem(z + n // 2, nz), n % 2, core))
+
+        @pl.loop(0, 2 * nz)
+        def _(n):
+            member = index(lax.rem(z + n // 2, nz), lax.rem(y + n, 2), 1 - core)
+            for h in (0, 1):
+                arrive(2, h, member)
+            sum_taps(member)
+
+    def compute_up():
         @pl.loop(0, c0 // 256)
         def _(n):
             at = pl.ds(pl.multiple_of(n * 256, 256), 256)
@@ -356,10 +424,13 @@
     compute_deep()
     second(2)
     third(2)
-    last(2)
+    last_up()
     compute_up()
-    for copy in started:
-        copy.wait_send()
+    for copy, when in started:
+        if when is True:
+            copy.wait_send()
+        else:
+            pl.when(when)(copy.wait_send)
 
 
 def fused_device(
@@ -379,29 +450,20 @@
         return jnp.pad(flat, ((0, 0), (0, -flat.shape[1] % lanes)))
 
     shards = [turned(weight, 256) for weight in (weight_top, weight_deep, weight_up)]
-    extended = with_halo(bases + 1, (("seq", 0),), 2 * EDGE + 2)
-    pairs = extended.reshape(rows + 2, 2)
-    window = jnp.stack(
-        [
-            jnp.stack(
-                [pairs[u // 2 : u // 2 + rows, u % 2] for u in range(q, q + TAPS)], axis=1
-            )
-            for q in range(2)
-        ]
-    )
-    codes = jnp.arange(1, 5, dtype=jnp.int32)
-    onehot = (window[..., None] == codes).astype(bf16).reshape(2 * rows, TAPS * 4)
-    onehot = jnp.pad(onehot, ((0, 0), (0, 128 - TAPS * 4)))
-    table = jnp.pad(stem_weight.reshape(TAPS * 4, c0), ((0, 128 - TAPS * 4), (0, 0)))
+    lane = jnp.arange(128, dtype=jnp.int32)
+    code = jnp.where((lane % 8 < 4) & (lane < 8 * TAPS), lane % 8, -1)
+    hot = (bases.reshape(half, 2).T[..., None] == code).astype(f32)
 
     k0, k1, k2 = (shard.shape[1] for shard in shards)
-    sends = 3 * (nz - 1 + 4 + 3 * (nz - 1) + 2 + 3 * (nz - 1) + nz - 1)
+    sends = 3 * (nz + 1 + 4 + 3 * (nz - 1) + 2 + 3 * (nz - 1) + nz - 1)
     out = pl.pallas_call(
         functools.partial(fused_kernel, nz, half),
         out_shape=jax.ShapeDtypeStruct((half, 2 * c0), bf16),
         in_specs=[pl.BlockSpec(memory_space=pltpu.VMEM)] * 8,
         out_specs=pl.BlockSpec(memory_space=pltpu.VMEM),
         scratch_shapes=[
+            pltpu.VMEM((2, half + 4 * EDGE, 128), f32),
+            pltpu.VMEM((128, c0), f32),
             pltpu.VMEM((c0, k0), bf16),
             pltpu.VMEM((members, weight_deep.shape[2], k1), bf16),
             pltpu.VMEM((c0, k2), bf16),
@@ -417,17 +479,18 @@
             pltpu.SemaphoreType.DMA((sends,)),
             pltpu.SemaphoreType.DMA((3, 2, members)),
             pltpu.SemaphoreType.DMA((3,)),
+            pltpu.SemaphoreType.DMA((5,)),
         ],
         compiler_params=pltpu.CompilerParams(
             collective_id=0, has_side_effects=True, vmem_limit_bytes=67043328
         ),
     )(
-        onehot,
-        table,
+        hot,
+        stem_weight,
         *shards,
-        gain_top.reshape(1, c0),
-        gain_deep.reshape(1, c0),
-        gain_up.reshape(1, c1),
+        gain_top,
+        gain_deep,
+        gain_up,
     )
     return out.reshape(count, c0)
 

time: 131 us -> 118 us (0.901)
  the two profiles are of different devices: /device:TPU:9 before, /device:TPU:0 now
where the time goes in v2:
time: 118 us; the launch traced here: 117 us
  Pallas kernels  109 us (92%)
  local copies, waits for them, and re-layouts  7.41 us (6%)
    pallas_call x1, Pallas kernels, fused_device(): pl.pallas_call(functools.partial(fused_kernel, nz, half), out_shape=jax.S...  109 us
    reshape x1, local copies, waits for them, and re-layouts, fused_device(): return out.reshape(count, c0)  2.95 us
    reshape x3, local copies, waits for them, and re-layouts, turned(): flat = weight.transpose(2, 0, 1).reshape(weight.shape[2], -1)  2.65 us

profile of v2, /device:TPU:0, one launch (start us, length us, event | category | flops | bytes accessed | tf_op | source)
XLA Modules:
  0.0 117.3 jit_solution(7376119595174768325)
XLA Ops:
  0.0 0.0 copy-start
  0.0 0.0 copy-start.1
  0.0 0.9 reshape.30
  0.9 0.1 copy.12
  1.0 1.8 %copy.16 = bf16[5,6,8,768]{3,2,0,1:T(8,128)(2,1)} copy(bf16[5,6,8,768]{3,2,1,0:T(8,128)(2,1)} %bitcast.16) | data formatting | bytes 737280 | tf_op jit(solution)/shard_map/reshape | solution.py:449
  2.8 0.9 compare_convert_fusion.hot_ref
  3.8 0.0 copy-done
  3.8 0.8 copy.17
  4.6 0.0 copy-done.1
  4.6 0.8 pad.4.up_ref
  5.4 108.9 %shard_map.82 = bf16[384,1536]{1,0:T(8,128)(2,1)} custom-call(f32[2,384,128]{2,1,0:T(8,128)} %compare_convert_fusion.hot_ref, bf16[5,4,768]{2,1,0:T(4,128)(2,1)} %stem_ref.1, bf16[48,3840]{1,0:T(8,128)(2,1)} %bitcast.12, bf16[56,3840]{1,0:T(8,128)(2,1)} %bitcast.10, bf16[48,4608]{1,0:T(8,128)(2,1)} %pad.4.up_ref, f32[768]{0:T(1024)} %gain_top_ref.1, ...), custom_call_target="tpu_custom_call" | custom-call | tf_op jit(solution)/shard_map/pallas_call | solution.py:459
  114.3 2.9 %reshape.34 = bf16[768,768]{1,0:T(8,128)(2,1)} reshape(bf16[384,1536]{1,0:T(8,128)(2,1)} %shard_map.82) | data formatting | bytes 2359296 | tf_op jit(solution)/shard_map/reshape | solution.py:495
  (2 shorter events, 0.0 us)
Async XLA Ops:
  0.0 3.8 %copy-start = (bf16[5,768,56]{1,2,0:T(8,128)(2,1)S(1)}, bf16[5,768,56]{1,2,0:T(8,128)(2,1)}, u32[]{:S(2)}) copy-start(bf16[5,768,56]{1,2,0:T(8,128)(2,1)} %param.11) | copy-start | bytes 1290244
  0.0 4.6 %copy-start.1 = (bf16[5,896,48]{1,2,0:T(8,128)(2,1)S(1)}, bf16[5,896,48]{1,2,0:T(8,128)(2,1)}, u32[]{:S(2)}) copy-start(bf16[5,896,48]{1,2,0:T(8,128)(2,1)} %param.12) | copy-start | bytes 1290244

commit v3 on v2

--- a/solution.py
+++ b/solution.py
@@ -123,8 +123,19 @@
     def index(z_at, y_at, core_at):
         return z_at * 4 + y_at * 2 + core_at
 
+    nearest = [
+        sorted(range(nz), key=lambda other: (abs(other - here), other))
+        for here in range(nz)
+    ]
+
     def away(k):
-        return lax.rem(z + k, nz)
+        found = jnp.int32(0)
+        for here in range(nz):
+            found = jnp.where(z == here, nearest[here][k], found)
+        return found
+
+    inner = (z > 0) & (z < nz - 1)
+    steps = ((z < nz - 1, 1), (z > 0, -1))
 
     mirror = (1 - g, s)
     across = (g, index(z, 1 - y, core))
@@ -175,9 +186,6 @@
 
     started = []
 
-    def near(k):
-        return (k == 1) & (z < nz - 1) | (k == nz - 1) & (z > 0)
-
     def send(stage, h, at, device, own=False, when=True):
         source = own_refs[stage].at[:, columns(stage, h)] if own else place(stage, h, at)
         copy = pltpu.make_async_remote_copy(
@@ -206,15 +214,20 @@
 
     own_copies = []
 
-    def begin(stage):
-        for k in range(1, nz):
-            target = (g, index(away(k), y, core))
-            send(stage, g, s, target, own=True)
-            if k in (1, nz - 1):
-                send(stage, 1 - g, s, target, own=True, when=near(k))
+    def along_z(stage, h):
+        for within, step in steps:
+            target = (g, index(jnp.clip(z + step, 0, nz - 1), y, core))
+            send(stage, h, s, target, own=True, when=within)
+
+    def own_across(stage):
         for h in (g, 1 - g):
             send(stage, h, s, across, own=True)
+
+    def own_sibling(stage):
+        for h in (g, 1 - g):
             send(stage, h, s, sibling, own=True)
+
+    def keep_own(stage):
         depth = own_refs[stage].shape[0]
         if stage == 1:
             target = full_deep.at[s]
@@ -227,12 +240,21 @@
 
     def first(stage):
         for k in range(1, nz):
-            at = index(away(k), y, core)
+            far = away(k)
+            at = index(far, y, core)
             arrive(stage, g, at)
-            if k in (1, nz - 1):
-                send(stage, g, at, mirror, when=jnp.logical_not(near(k)))
-            else:
+            onward = jnp.where(far < z, z + 1, z - 1)
+            send(
+                stage,
+                g,
+                at,
+                (g, index(jnp.clip(onward, 0, nz - 1), y, core)),
+                when=(onward >= 0) & (onward < nz),
+            )
+            if k > 2:
                 send(stage, g, at, mirror)
+            elif k == 2:
+                send(stage, g, at, mirror, when=jnp.logical_not(inner))
             send(stage, g, at, across)
             send(stage, g, at, sibling)
 
@@ -406,23 +428,34 @@
                     conv + skip[low : low + half, at]
                 ).astype(jnp.bfloat16)
 
-    begin(0)
-    begin(1)
-    begin(2)
+    along_z(0, g)
+    own_across(0)
+    own_sibling(0)
+    along_z(1, g)
+    for stage in range(3):
+        keep_own(stage)
     wide[...] = jnp.zeros_like(wide)
     prepare_top()
     first(0)
+    along_z(2, g)
+    along_z(0, 1 - g)
+    own_across(1)
+    own_sibling(1)
     second(0)
     first(1)
+    along_z(1, 1 - g)
+    own_across(2)
+    own_sibling(2)
     third(0)
+    second(1)
     last(0)
     compute_top()
-    second(1)
     first(2)
+    along_z(2, 1 - g)
     third(1)
+    second(2)
     last(1)
     compute_deep()
-    second(2)
     third(2)
     last_up()
     compute_up()
@@ -455,7 +488,7 @@
     hot = (bases.reshape(half, 2).T[..., None] == code).astype(f32)
 
     k0, k1, k2 = (shard.shape[1] for shard in shards)
-    sends = 3 * (nz + 1 + 4 + 3 * (nz - 1) + 2 + 3 * (nz - 1) + nz - 1)
+    sends = 3 * (4 + 4 + 4 * (nz - 1) + 2 + 3 * (nz - 1) + nz - 1)
     out = pl.pallas_call(
         functools.partial(fused_kernel, nz, half),
         out_shape=jax.ShapeDtypeStruct((half, 2 * c0), bf16),

time: 118 us -> 107 us (0.907)
  Pallas kernels: 109 us -> 98.2 us
    pallas_call x1, Pallas kernels: 109 us -> 98.2 us  [fused_device(): pl.pallas_call(functools.partial(fused_kernel, nz, half), out_shape=jax.S...]
where the time goes in v3:
time: 107 us
  Pallas kernels  98.2 us (92%)
  local copies, waits for them, and re-layouts  7.41 us (7%)
    pallas_call x1, Pallas kernels, fused_device(): pl.pallas_call(functools.partial(fused_kernel, nz, half), out_shape=jax.S...  98.2 us
    reshape x1, local copies, waits for them, and re-layouts, fused_device(): return out.reshape(count, c0)  2.95 us
    reshape x3, local copies, waits for them, and re-layouts, turned(): flat = weight.transpose(2, 0, 1).reshape(weight.shape[2], -1)  2.65 us

profile of v3, /device:TPU:0, one launch (start us, length us, event | category | flops | bytes accessed | tf_op | source)
XLA Modules:
  0.0 106.5 jit_solution(12007445545294949585)
XLA Ops:
  0.0 0.0 copy-start
  0.0 0.0 copy-start.1
  0.0 0.9 reshape.30
  0.9 0.1 copy.12
  1.0 1.8 %copy.16 = bf16[5,6,8,768]{3,2,0,1:T(8,128)(2,1)} copy(bf16[5,6,8,768]{3,2,1,0:T(8,128)(2,1)} %bitcast.16) | data formatting | bytes 737280 | tf_op jit(solution)/shard_map/reshape | solution.py:482
  2.8 0.9 compare_convert_fusion.hot_ref
  3.8 0.0 copy-done
  3.8 0.8 copy.17
  4.6 0.0 copy-done.1
  4.6 0.8 pad.4.up_ref
  5.4 98.2 %shard_map.82 = bf16[384,1536]{1,0:T(8,128)(2,1)} custom-call(f32[2,384,128]{2,1,0:T(8,128)} %compare_convert_fusion.hot_ref, bf16[5,4,768]{2,1,0:T(4,128)(2,1)} %stem_ref.1, bf16[48,3840]{1,0:T(8,128)(2,1)} %bitcast.12, bf16[56,3840]{1,0:T(8,128)(2,1)} %bitcast.10, bf16[48,4608]{1,0:T(8,128)(2,1)} %pad.4.up_ref, f32[768]{0:T(1024)} %gain_top_ref.1, ...), custom_call_target="tpu_custom_call" | custom-call | tf_op jit(solution)/shard_map/pallas_call | solution.py:492
  103.6 2.9 %reshape.34 = bf16[768,768]{1,0:T(8,128)(2,1)} reshape(bf16[384,1536]{1,0:T(8,128)(2,1)} %shard_map.82) | data formatting | bytes 2359296 | tf_op jit(solution)/shard_map/reshape | solution.py:528
  (2 shorter events, 0.0 us)
Async XLA Ops:
  0.0 3.8 %copy-start = (bf16[5,768,56]{1,2,0:T(8,128)(2,1)S(1)}, bf16[5,768,56]{1,2,0:T(8,128)(2,1)}, u32[]{:S(2)}) copy-start(bf16[5,768,56]{1,2,0:T(8,128)(2,1)} %param.11) | copy-start | bytes 1290244
  0.0 4.6 %copy-start.1 = (bf16[5,896,48]{1,2,0:T(8,128)(2,1)S(1)}, bf16[5,896,48]{1,2,0:T(8,128)(2,1)}, u32[]{:S(2)}) copy-start(bf16[5,896,48]{1,2,0:T(8,128)(2,1)} %param.12) | copy-start | bytes 1290244
